TPU v7x, 32 devices: a whole 2x2x4 slice. The times are simulated.
32 devices in a mesh: ep: 16 (over z, y, x), rep: 2 (over core).
Axes of the slice: x: 2, y: 2, z: 4, core: 2. Of those that a mesh axis runs over, the one named last changes fastest.
Arguments:
- tokens: bfloat16 [4096, 1024], P(('ep', 'rep')), may hold values from -6 to 6
- expert_ids: int32 [4096, 6], P(('ep', 'rep')), may hold values from 0 to 15, all different within a row; in each aligned block of 128 rows (0 to 127, 128 to 255, ...) at most 49 rows name the same one
- gate_weights: float32 [4096, 6], P(('ep', 'rep')), may hold values from 0.1 to 0.5
- cotangent: bfloat16 [4096, 1024], P(('ep', 'rep')), may hold values from -6 to 6
- w_gate: bfloat16 [16, 1024, 704], P('ep', 'rep'), may hold values from -0.1875 to 0.1875
- w_up: bfloat16 [16, 1024, 704], P('ep', 'rep'), may hold values from -0.1875 to 0.1875
- w_down: bfloat16 [16, 704, 1024], P('ep', None, 'rep'), may hold values from -0.21875 to 0.21875
Outputs:
- mixed_out: bfloat16 [4096, 1024], P(('ep', 'rep'))
- grad_up: float32 [16, 1024, 704], P('ep', 'rep')
- grad_down: float32 [16, 704, 1024], P('ep', None, 'rep')
Inputs may be any that keep to these rules, and one draw needn't show every extreme that they name: `expert_ids`: each token names 6 different experts. Of the tokens of one device, at most 49 name any one expert, and in every draw some expert is named by exactly 49 of some device's tokens.
All inputs are finite; a program needn't handle non-finite values.
Results may differ from a plain program's by a relative error of at most 0.012.
Values may be sent and summed in bfloat16 or wider, within the bound.
A program may use at most 128 MiB of HBM per device.

v0:
```python
import jax
import jax.numpy as jnp
from jax import lax
from jax.sharding import PartitionSpec as P


def local(tokens, expert_ids, gate_weights, cotangent, w_gate, w_up, w_down):
    ep_count = lax.axis_size("ep")
    tok_rows, feature_width = tokens.shape
    top_count = expert_ids.shape[1]
    slot_count = tok_rows * top_count // ep_count + 1
    pair_count = tok_rows * top_count
    flat_ids = expert_ids.reshape(pair_count)
    one_hot = (flat_ids[:, None] == jnp.arange(ep_count, dtype=jnp.int32)[None, :]).astype(
        jnp.int32
    )
    position = jnp.sum(one_hot * jnp.cumsum(one_hot, axis=0), axis=1) - 1
    target = flat_ids * slot_count + position
    owner_pair = (
        jnp.zeros((ep_count * slot_count,), jnp.int32)
        .at[target]
        .set(jnp.arange(pair_count, dtype=jnp.int32))
    )
    filled = jnp.zeros((ep_count * slot_count,), jnp.float32).at[target].set(1.0)
    source_row = owner_pair // top_count
    gate_flat = gate_weights.reshape(pair_count)
    send_rows = (tokens[source_row] * filled.astype(jnp.bfloat16)[:, None]).reshape(
        ep_count, slot_count, feature_width
    )
    pair_scale = gate_flat[owner_pair] * filled
    send_back = (pair_scale[:, None] * cotangent[source_row].astype(jnp.float32)).astype(
        jnp.bfloat16
    )
    send_back = send_back.reshape(ep_count, slot_count, feature_width)
    arrived, arrived_grad = (
        lax.all_to_all(send_rows, "ep", split_axis=0, concat_axis=0, tiled=True),
        lax.all_to_all(send_back, "ep", split_axis=0, concat_axis=0, tiled=True),
    )
    arrived_grad = arrived_grad.reshape(-1, feature_width)
    arrived = arrived.reshape(-1, feature_width)
    gate_shard = w_gate[0]
    up_shard = w_up[0]
    down_shard = w_down[0]
    columns = arrived
    gate_pre = jnp.dot(
        columns,
        lax.all_gather(gate_shard, "rep", axis=0, tiled=True),
        preferred_element_type=jnp.float32,
    )
    up_pre = jnp.dot(
        columns,
        lax.all_gather(up_shard, "rep", axis=0, tiled=True),
        preferred_element_type=jnp.float32,
    )
    gate_silu = jax.nn.silu(gate_pre)
    hidden = (gate_silu * up_pre).astype(jnp.bfloat16)
    expert_out = jnp.dot(
        hidden,
        lax.all_gather(down_shard, "rep", axis=1, tiled=True),
        preferred_element_type=jnp.float32,
    ).astype(jnp.bfloat16)
    returned = lax.all_to_all(
        expert_out.reshape(ep_count, slot_count, feature_width),
        "ep",
        split_axis=0,
        concat_axis=0,
        tiled=True,
    )
    returned = returned.reshape(ep_count * slot_count, feature_width)
    weighted = returned[target].astype(jnp.float32) * gate_flat[:, None]
    mixed_out = jnp.sum(weighted.reshape(tok_rows, top_count, feature_width), axis=1).astype(
        jnp.bfloat16
    )
    columns = arrived_grad
    hidden_grad = lax.dot_general(
        columns,
        lax.all_gather(down_shard, "rep", axis=1, tiled=True),
        (((1,), (1,)), ((), ())),
        preferred_element_type=jnp.float32,
    )
    up_grad = (hidden_grad * gate_silu).astype(jnp.bfloat16)
    part_up = lax.dot_general(
        arrived, up_grad, (((0,), (0,)), ((), ())), preferred_element_type=jnp.float32
    )
    part_down = lax.dot_general(
        hidden, arrived_grad, (((0,), (0,)), ((), ())), preferred_element_type=jnp.float32
    )
    grad_up, grad_down = (
        lax.psum_scatter(
            part_up.astype(jnp.bfloat16), "rep", scatter_dimension=0, tiled=True
        ).astype(jnp.float32),
        lax.psum_scatter(
            part_down.astype(jnp.bfloat16), "rep", scatter_dimension=1, tiled=True
        ).astype(jnp.float32),
    )
    return (mixed_out, grad_up[None], grad_down[None])


def solution(mesh):
    in_specs = (
        P(("ep", "rep"), None),
        P(("ep", "rep"), None),
        P(("ep", "rep"), None),
        P(("ep", "rep"), None),
        P("ep", "rep", None),
        P("ep", "rep", None),
        P("ep", None, "rep"),
    )
    out_specs = (P(("ep", "rep"), None), P("ep", "rep", None), P("ep", None, "rep"))
    return jax.shard_map(local, mesh=mesh, in_specs=in_specs, out_specs=out_specs, check_vma=False)
```

profile of v0, /device:TPU:0, one launch (start us, length us, event | category | flops | bytes accessed | tf_op | source)
XLA Modules:
  0.0 215.4 jit_solution(1743030145699589056)
XLA Ops:
  11.4 3.4 %scatter_custom_fusion = s32[784]{0:T(1024)S(1)} fusion(s32[768]{0:T(1024)S(1)} %fusion.13, s32[768]{0:T(1024)S(1)} %iota.11, s32[]{:T(128)} %constant.10.clone.1), kind=kCustom, calls=%fused_computation.45 | custom fusion | bytes 3140 | tf_op jit(solution)/shard_map/scatter | solution.py:22
  15.8 3.5 %gather_fusion.2 = f32[784]{0:T(1024)S(1)} fusion(f32[768]{0:T(1024)S(1)} %reshape.104, s32[1024]{0:T(1024)S(1)} %get-tuple-element.7), kind=kCustom, calls=%fused_computation.2 | custom fusion | bytes 9408 | tf_op jit(solution)/shard_map/gather | solution.py:30
  19.2 3.4 %scatter_custom_fusion.1 = f32[784]{0:T(1024)S(1)} fusion(s32[768]{0:T(1024)S(1)} %fusion.13, f32[768]{0:T(1024)S(1)} %broadcast.81, f32[]{:T(128)} %constant.32.clone.1), kind=kCustom, calls=%fused_computation.41 | custom fusion | bytes 3140 | tf_op jit(solution)/shard_map/scatter | solution.py:24
  22.7 4.1 %gather_fusion = bf16[784,1024]{1,0:T(8,128)(2,1)} fusion(bf16[128,1024]{1,0:T(8,128)(2,1)S(1)} %copy-done, s32[1024]{0:T(1024)S(1)} %get-tuple-element.8), kind=kCustom, calls=%fused_computation | custom fusion | bytes 3214400 | tf_op jit(solution)/shard_map/gather | solution.py:27
  30.0 8.5 %all-to-all-start = ((bf16[16,49,1024]{2,1,0:T(8,128)(2,1)}), bf16[16,49,1024]{2,1,0:T(8,128)(2,1)S(1)}, u32[]{:S(2)}, u32[]{:S(2)}) async-start(bf16[16,49,1024]{2,1,0:T(8,128)(2,1)} %broadcast_multiply_fusion), calls=%async_computation | async-start | bytes 3670016 | tf_op jit(solution)/shard_map/all_to_all | solution.py:36
  39.3 4.1 %gather_fusion.3 = bf16[784,1024]{1,0:T(8,128)(2,1)} fusion(bf16[128,1024]{1,0:T(8,128)(2,1)S(1)} %copy-done.1, s32[1024]{0:T(1024)S(1)} %get-tuple-element.8), kind=kCustom, calls=%fused_computation.3 | custom fusion | bytes 3214400 | tf_op jit(solution)/shard_map/gather | solution.py:31
  43.4 3.2 %reshape.107 = f32[16,49,1024]{2,1,0:T(8,128)} reshape(bf16[784,1024]{1,0:T(8,128)(2,1)} %gather_fusion.3) | data formatting | bytes 4816896 | tf_op jit(solution)/shard_map/convert_element_type | solution.py:31
  46.6 3.7 %multiply_convert_fusion = bf16[16,49,1024]{2,1,0:T(8,128)(2,1)} fusion(f32[16,49,1024]{2,1,0:T(8,128)} %reshape.107, f32[16,49]{1,0:T(8,128)S(1)} %mul.75), kind=kLoop, calls=%fused_computation.7 | loop fusion | flops 1605632 | bytes 4820032 | tf_op jit(solution)/shard_map/convert_element_type | solution.py:31
  50.3 26.7 %all-to-all-done = bf16[16,49,1024]{2,1,0:T(8,128)(2,1)S(1)} async-done(((bf16[16,49,1024]{2,1,0:T(8,128)(2,1)}), bf16[16,49,1024]{2,1,0:T(8,128)(2,1)S(1)}, u32[]{:S(2)}, u32[]{:S(2)}) %all-to-all-start) | async-done | bytes 1605664 | tf_op jit(solution)/shard_map/all_to_all | solution.py:36
  77.0 9.0 %all-to-all-start.2 = ((bf16[16,49,1024]{2,1,0:T(8,128)(2,1)}), bf16[16,49,1024]{2,1,0:T(8,128)(2,1)}, u32[]{:S(2)}, u32[]{:S(2)}) async-start(bf16[16,49,1024]{2,1,0:T(8,128)(2,1)} %multiply_convert_fusion), calls=%async_computation.2 | async-start | bytes 3670016 | tf_op jit(solution)/shard_map/all_to_all | solution.py:37
  89.2 34.9 %all-to-all-done.2 = bf16[16,49,1024]{2,1,0:T(8,128)(2,1)} async-done(((bf16[16,49,1024]{2,1,0:T(8,128)(2,1)}), bf16[16,49,1024]{2,1,0:T(8,128)(2,1)}, u32[]{:S(2)}, u32[]{:S(2)}) %all-to-all-start.2) | async-done | bytes 1605664 | tf_op jit(solution)/shard_map/all_to_all | solution.py:37
  124.1 1.7 reshape.105
  125.9 4.5 %divide_multiply_fusion = f32[784,704]{1,0:T(8,128)} fusion(bf16[784,1024]{1,0:T(8,128)(2,1)S(1)} %copy-done.2, bf16[1,1024,704]{1,2,0:T(8,128)(2,1)} %all-gather.7.cloned.1.call-done), kind=kOutput, calls=%fused_computation.10 | convolution fusion | flops 1132572672 | bytes 5255168 | tf_op jit(solution)/shard_map/dot_general | solution.py:45
  130.4 8.6 %convolution_convert_fusion.2 = bf16[1024,704]{0,1:T(8,128)(2,1)} fusion(bf16[784,1024]{1,0:T(8,128)(2,1)S(1)} %copy-done.2, f32[784,704]{1,0:T(8,128)} %divide_multiply_fusion, bf16[784,1024]{1,0:T(8,128)(2,1)S(1)} %reshape.105, bf16[1,704,1024]{2,1,0:T(8,128)(2,1)} %all-gather.11.cloned.1.call-done), kind=kOutput, calls=%fused_computation.13 | convolution fusion | flops 2262554624 | bytes 8302592 | tf_op jit(solution)/shard_map/dot_general | solution.py:82
  139.1 3.6 %multiply_convert_fusion.2 = bf16[784,704]{1,0:T(8,128)(2,1)S(1)} fusion(f32[784,704]{1,0:T(8,128)} %divide_multiply_fusion, bf16[784,1024]{1,0:T(8,128)(2,1)S(1)} %copy-done.2, bf16[1,1024,704]{1,2,0:T(8,128)(2,1)} %all-gather.9.cloned.1.call-done), kind=kOutput, calls=%fused_computation.9 | convolution fusion | flops 1131468800 | bytes 6359040 | tf_op jit(solution)/shard_map/dot_general | solution.py:50
  143.6 2.8 %convolution_convert_fusion.1 = bf16[704,1024]{1,0:T(8,128)(2,1)} fusion(bf16[784,704]{1,0:T(8,128)(2,1)S(1)} %multiply_convert_fusion.2, bf16[784,1024]{1,0:T(8,128)(2,1)S(1)} %reshape.105), kind=kOutput, calls=%fused_computation.12 | convolution fusion | flops 1131085824 | bytes 4151296 | tf_op jit(solution)/shard_map/dot_general | solution.py:85
  146.5 3.4 %convolution_convert_fusion = bf16[784,1024]{1,0:T(8,128)(2,1)S(1)} fusion(bf16[784,704]{1,0:T(8,128)(2,1)} %copy-done.3, bf16[1,704,1024]{2,1,0:T(8,128)(2,1)} %all-gather.11.cloned.1.call-done), kind=kOutput, calls=%fused_computation.11 | convolution fusion | flops 1131167744 | bytes 4151296 | tf_op jit(solution)/shard_map/dot_general | solution.py:57
  151.4 8.3 %all-to-all-start.1 = ((bf16[16,49,1024]{2,1,0:T(8,128)(2,1)}), bf16[16,49,1024]{2,1,0:T(8,128)(2,1)}, u32[]{:S(2)}, u32[]{:S(2)}) async-start(bf16[16,49,1024]{2,1,0:T(8,128)(2,1)} %reshape.102), calls=%async_computation.1 | async-start | bytes 3670016 | tf_op jit(solution)/shard_map/all_to_all | solution.py:62
  159.8 2.5 %bitcast_convert_fusion.1 = f32[1,512,704]{1,2,0:T(8,128)} fusion(bf16[512,704]{0,1:T(8,128)(2,1)} %reduce-scatter.3.cloned.1.call-done), kind=kLoop, calls=%fused_computation.21 | loop fusion | flops 360448 | bytes 2162688 | tf_op jit(solution)/shard_map/broadcast_in_dim | solution.py:96
  163.0 2.4 %bitcast_convert_fusion = f32[1,704,512]{2,1,0:T(8,128)} fusion(bf16[704,512]{1,0:T(8,128)(2,1)} %reduce-scatter.5.cloned.1.call-done), kind=kLoop, calls=%fused_computation.20 | loop fusion | flops 360448 | bytes 2162688 | tf_op jit(solution)/shard_map/broadcast_in_dim | solution.py:96
  165.4 32.5 %all-to-all-done.1 = bf16[16,49,1024]{2,1,0:T(8,128)(2,1)} async-done(((bf16[16,49,1024]{2,1,0:T(8,128)(2,1)}), bf16[16,49,1024]{2,1,0:T(8,128)(2,1)}, u32[]{:S(2)}, u32[]{:S(2)}) %all-to-all-start.1) | async-done | bytes 1605664 | tf_op jit(solution)/shard_map/all_to_all | solution.py:62
  199.6 2.8 %gather_fusion.1 = bf16[768,1024]{1,0:T(8,128)(2,1)S(1)} fusion(bf16[784,1024]{1,0:T(8,128)(2,1)S(1)} %reshape.103, s32[1024]{0:T(1024)S(1)} %pad_clamp_fusion.1), kind=kCustom, calls=%fused_computation.1 | custom fusion | bytes 3148800 | tf_op jit(solution)/shard_map/gather | solution.py:70
  202.5 2.1 reshape.106
  204.6 4.3 %multiply_reduce_fusion = bf16[128,1024]{1,0:T(8,128)(2,1)} fusion(f32[128,6,1024]{2,1,0:T(8,128)} %reshape.106, f32[128,6]{1,0:T(8,128)S(1)} %copy.15), kind=kLoop, calls=%fused_computation.6 | loop fusion | flops 1441792 | bytes 3410944 | tf_op jit(solution)/shard_map/reduce_sum | solution.py:71
  (51 shorter events, 17.4 us)
Async XLA Ops:
  7.2 15.6 %copy-start = (bf16[128,1024]{1,0:T(8,128)(2,1)S(1)}, bf16[128,1024]{1,0:T(8,128)(2,1)}, u32[]{:S(2)}) copy-start(bf16[128,1024]{1,0:T(8,128)(2,1)} %param.7) | copy-start | bytes 786436
  30.0 9.3 %copy-start.1 = (bf16[128,1024]{1,0:T(8,128)(2,1)S(1)}, bf16[128,1024]{1,0:T(8,128)(2,1)}, u32[]{:S(2)}) copy-start(bf16[128,1024]{1,0:T(8,128)(2,1)} %param.10) | copy-start | bytes 786436
  30.0 47.0 %all-to-all-start = ((bf16[16,49,1024]{2,1,0:T(8,128)(2,1)}), bf16[16,49,1024]{2,1,0:T(8,128)(2,1)S(1)}, u32[]{:S(2)}, u32[]{:S(2)}) async-start(bf16[16,49,1024]{2,1,0:T(8,128)(2,1)} %broadcast_multiply_fusion), calls=%async_computation | async-start | bytes 3670016 | tf_op jit(solution)/shard_map/all_to_all | solution.py:36
  38.4 87.4 %all-gather.7.cloned.1.call-start = ((), (), s32[]{:S(2)}) async-start(), calls=%async_computation.7 | async-start | bytes 2162688 | tf_op jit(solution)/shard_map/all_gather | solution.py:47
  77.0 47.1 %all-to-all-start.2 = ((bf16[16,49,1024]{2,1,0:T(8,128)(2,1)}), bf16[16,49,1024]{2,1,0:T(8,128)(2,1)}, u32[]{:S(2)}, u32[]{:S(2)}) async-start(bf16[16,49,1024]{2,1,0:T(8,128)(2,1)} %multiply_convert_fusion), calls=%async_computation.2 | async-start | bytes 3670016 | tf_op jit(solution)/shard_map/all_to_all | solution.py:37
  86.0 44.4 %all-gather.11.cloned.1.call-start = ((), (), s32[]{:S(2)}) async-start(), calls=%async_computation.9 | async-start | bytes 2162688 | tf_op jit(solution)/shard_map/all_gather | solution.py:59
  86.7 52.3 %all-gather.9.cloned.1.call-start = ((), (), s32[]{:S(2)}) async-start(), calls=%async_computation.8 | async-start | bytes 2162688 | tf_op jit(solution)/shard_map/all_gather | solution.py:52
  87.4 72.4 %reduce-scatter.3.cloned.1.call-start = ((), (), s32[]{:S(2)}) async-start(), calls=%async_computation.5 | async-start | bytes 2162688 | tf_op jit(solution)/shard_map/reduce_scatter | solution.py:89
  89.2 36.7 %copy-start.2 = (bf16[784,1024]{1,0:T(8,128)(2,1)S(1)}, bf16[784,1024]{1,0:T(8,128)(2,1)}, u32[]{:S(2)}) copy-start(bf16[784,1024]{1,0:T(8,128)(2,1)} %reshape.101) | copy-start | bytes 4816900
  139.0 24.0 %reduce-scatter.5.cloned.1.call-start = ((), (), s32[]{:S(2)}) async-start(), calls=%async_computation.6 | async-start | bytes 2162688 | tf_op jit(solution)/shard_map/reduce_scatter | solution.py:92
  142.6 1.0 copy-start.3
  151.4 46.5 %all-to-all-start.1 = ((bf16[16,49,1024]{2,1,0:T(8,128)(2,1)}), bf16[16,49,1024]{2,1,0:T(8,128)(2,1)}, u32[]{:S(2)}, u32[]{:S(2)}) async-start(bf16[16,49,1024]{2,1,0:T(8,128)(2,1)} %reshape.102), calls=%async_computation.1 | async-start | bytes 3670016 | tf_op jit(solution)/shard_map/all_to_all | solution.py:62
Sparse Core Ops, SparseCore 0:
  40.8 10.8 all-gather.6
  88.3 10.8 all-gather.10
  100.8 10.7 all-gather.8
  139.1 11.6 reduce-scatter.2
  152.9 10.0 reduce-scatter.4
where the time goes:
time: 219 us; the launch traced here: 215 us
  waiting for transfers between devices  96.9 us (44%)
  local copies, waits for them, and re-layouts  38.5 us (18%)
  starting transfers between devices  26.2 us (12%)
  matrix products  22.9 us (10%)
  other arithmetic  16.9 us (8%)
  between operations  14 us (6%)
    all_to_all x1, waiting for transfers between devices, local(): lax.all_to_all(send_back, 'ep', split_axis=0, concat_axis=0, tiled=True)  34.9 us
    all_to_all x1, waiting for transfers between devices, local(): lax.all_to_all(expert_out.reshape(ep_count, slot_count, feature_width), '...  32.5 us
    all_to_all x1, waiting for transfers between devices, local(): lax.all_to_all(send_rows, 'ep', split_axis=0, concat_axis=0, tiled=True)  26.7 us
    all_to_all x1, starting transfers between devices, local(): lax.all_to_all(send_back, 'ep', split_axis=0, concat_axis=0, tiled=True)  8.97 us
    dot_general x1, matrix products, local(): lax.dot_general(arrived, up_grad, (((0,), (0,)), ((), ())), preferred_ele...  8.57 us
    all_to_all x1, starting transfers between devices, local(): lax.all_to_all(send_rows, 'ep', split_axis=0, concat_axis=0, tiled=True)  8.47 us
    all_to_all x1, starting transfers between devices, local(): lax.all_to_all(expert_out.reshape(ep_count, slot_count, feature_width), '...  8.34 us
    gather x2, local copies, waits for them, and re-layouts, local(): tokens[source_row] * filled.astype(jnp.bfloat16)[:, None]  5.79 us
  transfers between devices with their start and end apart: 8, of which 4 were waited for; matrix products, arithmetic and copies ran while one was open for 20% of the time, Pallas kernels for 0%

commit v1 on v0

v1 whole, which is shorter than its diff:
```python
import functools

import jax
import jax.numpy as jnp
from jax import lax
from jax.experimental import pallas as pl
from jax.experimental.pallas import tpu as pltpu
from jax.sharding import PartitionSpec as P

MESH = pl.DeviceIdType.MESH
F32 = jnp.float32
BF16 = jnp.bfloat16


def rows_of(count, unit):
    return -(-count // unit) * unit


def outer_of(ep_count):
    outer = 1
    while outer * outer < ep_count and ep_count % (outer * 2) == 0:
        outer *= 2
    return outer


def contract_rows(lhs, rhs):
    return lax.dot_general(lhs, rhs, (((0,), (0,)), ((), ())), preferred_element_type=F32)


def kernel(
    dims,
    meta_ref, tok_ref, cot_ref, wg_ref, wu_ref, wd_ref,
    mixed_ref, gup_ref, gdn_ref,
    metab, tokb, cotb, wgb, wub, wdb,
    slotb, gateb, pick, scale, mixhi, mixlo,
    sendx, recvx, sendg, recvg, sendo, recvo,
    gacc, uacc, hid, upg,
    comb, macc, sendz, recvz, supb, rupb, sdnb, rdnb,
    lsem, zs, zr, ps, pr, ys, yr, ws, wr, gs, gr,
):
    A, B, R, C, T, K, KP, cap, S, D, DC, H = dims
    CR = C // R
    ep = lax.axis_index("ep")
    rep = lax.axis_index("rep")
    oa, ob = ep // B, ep % B

    def out_peer(j):
        return {"ep": lax.rem(oa + j, A) * B + ob}

    def in_peer(j):
        return {"ep": oa * B + lax.rem(ob + j + B, B)}

    def rep_peer(j):
        return {"rep": lax.rem(rep + j, R)}

    peers = (
        [out_peer(j) for j in range(1, A)]
        + [in_peer(j) for j in range(1, B)]
        + [rep_peer(j) for j in range(1, R)]
    )

    def remote(src, dst, ssem, rsem, peer):
        copy = pltpu.make_async_remote_copy(
            src_ref=src, dst_ref=dst, send_sem=ssem, recv_sem=rsem,
            device_id=peer, device_id_type=MESH,
        )
        copy.start()
        return copy

    started = []
    local = {}

    def keep(src, dst, index):
        copy = pltpu.make_async_copy(src, dst, lsem.at[index])
        copy.start()
        return copy

    def cols(c):
        return pl.ds(c * DC, DC)

    for c in range(C):
        local["t", c] = keep(tok_ref.at[:, cols(c)], tokb.at[c, oa], c)
    local["g"] = keep(wg_ref, wgb.at[rep], 2 * C)
    local["u"] = keep(wu_ref, wub.at[rep], 2 * C + 1)
    local["d"] = keep(wd_ref, wdb.at[rep], 2 * C + 2)
    for c in range(C):
        local["c", c] = keep(cot_ref.at[:, cols(c)], cotb.at[c, oa], C + c)

    barrier = pltpu.get_barrier_semaphore()
    for peer in peers:
        pl.semaphore_signal(barrier, inc=1, device_id=peer, device_id_type=MESH)
    pl.semaphore_wait(barrier, len(peers))

    zc = {}
    for j in range(1, A):
        zc["m", j] = remote(meta_ref, metab.at[oa], zs.at[2 * C, j], zr.at[2 * C, j], out_peer(j))
    for c in range(C):
        for j in range(1, A):
            zc["t", c, j] = remote(
                tok_ref.at[:, cols(c)], tokb.at[c, oa], zs.at[c, j], zr.at[c, j], out_peer(j)
            )
    wc = {}
    for n, (src, dst) in enumerate(((wg_ref, wgb), (wu_ref, wub), (wd_ref, wdb))):
        for j in range(1, R):
            wc[n, j] = remote(src, dst.at[rep], ws.at[n, j], wr.at[n, j], rep_peer(j))
    for c in range(C):
        for j in range(1, A):
            zc["c", c, j] = remote(
                cot_ref.at[:, cols(c)], cotb.at[c, oa], zs.at[C + c, j], zr.at[C + c, j], out_peer(j)
            )
    started += list(zc.values()) + list(wc.values())

    metab[oa] = meta_ref[...]
    BP = slotb.shape[0]
    row = lax.broadcasted_iota(jnp.int32, (BP, T), 0)
    named = jnp.where(row < B, oa * B + lax.rem(ob + row, B), -1).astype(F32)
    earlier = (
        lax.broadcasted_iota(jnp.int32, (T, T), 0) < lax.broadcasted_iota(jnp.int32, (T, T), 1)
    ).astype(F32).astype(BF16)
    for j in range(1, A):
        zc["m", j].wait_recv()
    for a in range(A):
        member = jnp.zeros((BP, T), F32)
        weight = jnp.zeros((BP, T), F32)
        for k in range(K):
            same = metab[a, k : k + 1, :] == named
            member = member + jnp.where(same, 1.0, 0.0)
            weight = weight + jnp.where(same, metab[a, KP + k : KP + k + 1, :], 0.0)
        place = jnp.dot(member.astype(BF16), earlier, preferred_element_type=F32)
        slotb[:, a * T : (a + 1) * T] = jnp.where(member > 0.5, place + float(a * cap), -1.0)
        gateb[:, a * T : (a + 1) * T] = weight
    slot_id = lax.broadcasted_iota(jnp.int32, (S, A * T), 0).astype(F32)
    for b in range(B):
        hit = slotb[b : b + 1, :] == slot_id
        pick[b] = jnp.where(hit, 1.0, 0.0).astype(BF16)
        mix = jnp.where(hit, gateb[b : b + 1, :], 0.0)
        scale[b] = jnp.sum(mix, axis=1, keepdims=True)
        high = mix.astype(BF16)
        mixhi[b] = high
        mixlo[b] = (mix - high.astype(F32)).astype(BF16)

    pc = {}

    def pack_rows(c):
        local["t", c].wait()
        for j in range(1, A):
            zc["t", c, j].wait_recv()
        source = tokb[c].reshape(A * T, DC)
        for j in list(range(1, B)) + [0]:
            block = jnp.dot(pick[j], source, preferred_element_type=F32).astype(BF16)
            if j == 0:
                recvx[c, 0] = block
            else:
                sendx[c, j] = block
                pc["x", c, j] = remote(
                    sendx.at[c, j], recvx.at[c, j], ps.at[c, j], pr.at[c, j], in_peer(j)
                )

    def pack_grads(c):
        local["c", c].wait()
        for j in range(1, A):
            zc["c", c, j].wait_recv()
        source = cotb[c].reshape(A * T, DC)
        for j in list(range(1, B)) + [0]:
            block = jnp.dot(pick[j], source, preferred_element_type=F32)
            block = (block * scale[j]).astype(BF16)
            if j == 0:
                recvg[c, 0] = block
            else:
                sendg[c, j] = block
                pc["g", c, j] = remote(
                    sendg.at[c, j], recvg.at[c, j], ps.at[C + c, j], pr.at[C + c, j], in_peer(j)
                )

    for c in range(C):
        pack_rows(c)

    local["g"].wait()
    local["u"].wait()
    for j in range(1, R):
        wc[0, j].wait_recv()
        wc[1, j].wait_recv()
    for c in range(C):
        part = pl.ds((c % CR) * DC, DC)
        for j in range(1, B):
            pc["x", c, j].wait_recv()

        def gate_up(b, _, c=c, part=part):
            rows = recvx[c, b]
            gate = jnp.dot(rows, wgb[c // CR, part, :], preferred_element_type=F32)
            up = jnp.dot(rows, wub[c // CR, part, :], preferred_element_type=F32)
            if c > 0:
                gate = gate + gacc[b]
                up = up + uacc[b]
            if c < C - 1:
                gacc[b] = gate
                uacc[b] = up
            else:
                silu = gate / (1.0 + jnp.exp(-gate))
                gacc[b] = silu
                hid[b] = (silu * up).astype(BF16)
            return 0

        lax.fori_loop(0, B, gate_up, 0)
        pack_grads(c)

    local["d"].wait()
    for j in range(1, R):
        wc[2, j].wait_recv()
    for c in range(C):
        part = pl.ds((c % CR) * DC, DC)
        for j in list(range(1, B)) + [0]:
            block = jnp.dot(
                hid[j], wdb[c // CR, :, part], preferred_element_type=F32
            ).astype(BF16)
            if j == 0:
                recvo[c, 0] = block
            else:
                sendo[c, j] = block
                pc["o", c, j] = remote(
                    sendo.at[c, j], recvo.at[c, j],
                    ps.at[2 * C + c, j], pr.at[2 * C + c, j], in_peer(-j),
                )

    for c in range(C):
        part = pl.ds((c % CR) * DC, DC)
        for j in range(1, B):
            pc["g", c, j].wait_recv()

        def back(b, _, c=c, part=part):
            value = lax.dot_general(
                recvg[c, b], wdb[c // CR, :, part], (((1,), (1,)), ((), ())),
                preferred_element_type=F32,
            )
            if c > 0:
                value = value + uacc[b]
            if c < C - 1:
                uacc[b] = value
            else:
                upg[b] = (value * gacc[b]).astype(BF16)
            return 0

        lax.fori_loop(0, B, back, 0)

    hidden = lambda: hid[...].reshape(B * S, H)
    up_grad = lambda: upg[...].reshape(B * S, H)
    gc = {}
    for j in range(1, R):
        peer = lax.rem(rep + j, R)
        for i in range(CR):
            block = contract_rows(recvx[peer * CR + i].reshape(B * S, DC), up_grad())
            supb[j, i * DC : (i + 1) * DC, :] = block.astype(BF16)
        gc[0, j] = remote(supb.at[j], rupb.at[j], gs.at[0, j], gr.at[0, j], rep_peer(j))
        for i in range(CR):
            block = contract_rows(hidden(), recvg[peer * CR + i].reshape(B * S, DC))
            sdnb[j, :, i * DC : (i + 1) * DC] = block.astype(BF16)
        gc[1, j] = remote(sdnb.at[j], rdnb.at[j], gs.at[1, j], gr.at[1, j], rep_peer(j))

    yc = {}

    def combine(c):
        for j in range(1, B):
            pc["o", c, j].wait_recv()
        rows = recvo[c].reshape(B * S, DC)
        total = contract_rows(mixhi[...].reshape(B * S, A * T), rows)
        total = total + contract_rows(mixlo[...].reshape(B * S, A * T), rows)
        comb[...] = total.reshape(A, T, DC)
        sendz[c] = total.astype(BF16).reshape(A, T, DC)
        macc[c] = comb[oa]
        for j in range(1, A):
            yc[c, j] = remote(
                sendz.at[c, lax.rem(oa + j, A)], recvz.at[c, j],
                ys.at[c, j], yr.at[c, j], out_peer(j),
            )

    for c in range(C):
        combine(c)

    for i in range(CR):
        block = contract_rows(recvx[rep * CR + i].reshape(B * S, DC), up_grad())
        gup_ref[i * DC : (i + 1) * DC, :] = block.astype(BF16).astype(F32)
        block = contract_rows(hidden(), recvg[rep * CR + i].reshape(B * S, DC))
        gdn_ref[:, i * DC : (i + 1) * DC] = block.astype(BF16).astype(F32)
    for j in range(1, R):
        gc[0, j].wait_recv()
        gup_ref[...] += rupb[j].astype(F32)
        gc[1, j].wait_recv()
        gdn_ref[...] += rdnb[j].astype(F32)

    for c in range(C):
        total = macc[c]
        for j in range(1, A):
            yc[c, j].wait_recv()
            total = total + recvz[c, j].astype(F32)
        mixed_ref[:, c * DC : (c + 1) * DC] = total.astype(BF16)

    started += list(pc.values()) + list(gc.values()) + list(yc.values())
    for copy in started:
        copy.wait_send()


def local(tokens, expert_ids, gate_weights, cotangent, w_gate, w_up, w_down):
    ep_count, R = lax.axis_size("ep"), lax.axis_size("rep")
    T, D = tokens.shape
    K = expert_ids.shape[1]
    H = w_gate.shape[2]
    cap = T * K // ep_count + 1
    A = outer_of(ep_count)
    B = ep_count // A
    S = rows_of(A * cap, 16)
    DR = D // R
    DC = DR // 2 if DR % 256 == 0 else DR
    C = D // DC
    KP = rows_of(K, 8)
    BP = rows_of(B, 16)
    meta = jnp.concatenate(
        [
            jnp.pad(expert_ids.T.astype(F32), ((0, KP - K), (0, 0)), constant_values=-2.0),
            jnp.pad(gate_weights.T, ((0, KP - K), (0, 0))),
        ]
    )
    dims = (A, B, R, C, T, K, KP, cap, S, D, DC, H)
    vmem, dma = pltpu.VMEM, pltpu.SemaphoreType.DMA
    anywhere = pl.BlockSpec(memory_space=pl.ANY)
    inside = pl.BlockSpec(memory_space=pltpu.VMEM)
    blocks = vmem((C, B, S, DC), BF16)
    mixed, gup, gdn = pl.pallas_call(
        functools.partial(kernel, dims),
        out_shape=(
            jax.ShapeDtypeStruct((T, D), BF16),
            jax.ShapeDtypeStruct((DR, H), F32),
            jax.ShapeDtypeStruct((H, DR), F32),
        ),
        in_specs=[inside] + [anywhere] * 5,
        out_specs=[inside] * 3,
        scratch_shapes=[
            vmem((A, 2 * KP, T), F32),
            vmem((C, A, T, DC), BF16),
            vmem((C, A, T, DC), BF16),
            vmem((R, DR, H), BF16),
            vmem((R, DR, H), BF16),
            vmem((R, H, DR), BF16),
            vmem((BP, A * T), F32),
            vmem((BP, A * T), F32),
            vmem((B, S, A * T), BF16),
            vmem((B, S, 1), F32),
            vmem((B, S, A * T), BF16),
            vmem((B, S, A * T), BF16),
            blocks, blocks, blocks, blocks, blocks, blocks,
            vmem((B, S, H), F32),
            vmem((B, S, H), F32),
            vmem((B, S, H), BF16),
            vmem((B, S, H), BF16),
            vmem((A, T, DC), F32),
            vmem((C, T, DC), F32),
            vmem((C, A, T, DC), BF16),
            vmem((C, A, T, DC), BF16),
            vmem((R, DR, H), BF16),
            vmem((R, DR, H), BF16),
            vmem((R, H, DR), BF16),
            vmem((R, H, DR), BF16),
            dma((2 * C + 3,)),
            dma((2 * C + 1, A)), dma((2 * C + 1, A)),
            dma((3 * C, B)), dma((3 * C, B)),
            dma((C, A)), dma((C, A)),
            dma((3, R)), dma((3, R)),
            dma((2, R)), dma((2, R)),
        ],
        compiler_params=pltpu.CompilerParams(
            collective_id=0, has_side_effects=True, vmem_limit_bytes=62 * 1024 * 1024
        ),
    )(meta, tokens, cotangent, w_gate[0], w_up[0], w_down[0])
    return mixed, gup[None], gdn[None]


def solution(mesh):
    in_specs = (
        P(("ep", "rep"), None),
        P(("ep", "rep"), None),
        P(("ep", "rep"), None),
        P(("ep", "rep"), None),
        P("ep", "rep", None),
        P("ep", "rep", None),
        P("ep", None, "rep"),
    )
    out_specs = (P(("ep", "rep"), None), P("ep", "rep", None), P("ep", None, "rep"))
    return jax.shard_map(local, mesh=mesh, in_specs=in_specs, out_specs=out_specs, check_vma=False)
```

time: 219 us -> 110 us (0.50); the launches traced: 215 us -> 109 us
  Pallas kernels: 0 us -> 98.4 us
  waiting for transfers between devices: 96.9 us -> 0 us
  local copies, waits for them, and re-layouts: 38.5 us -> 8.32 us
  starting transfers between devices: 26.2 us -> 0 us
  matrix products: 22.9 us -> 0 us
  other arithmetic: 16.9 us -> 2.05 us
  between operations: 14 us -> 0.67 us
    pallas_call x0 -> x1, Pallas kernels: none -> 98.4 us  [local(): pl.pallas_call(functools.partial(kernel, dims), out_shape=(jax.ShapeDtype...]
    all_to_all x3 -> x0, waiting for transfers between devices: 94.1 us -> none  [the longest x1 34.9 us: local(): lax.all_to_all(send_back, 'ep', split_axis=0, concat_axis=0, tiled=True)]
    all_to_all x3 -> x0, starting transfers between devices: 25.8 us -> none  [the longest x1 8.97 us: local(): lax.all_to_all(send_back, 'ep', split_axis=0, concat_axis=0, tiled=True)]
    dot_general x5 -> x0, matrix products: 22.9 us -> none  [the longest x1 8.57 us: local(): lax.dot_general(arrived, up_grad, (((0,), (0,)), ((), ())), preferred_ele...]
    gather x5 -> x0, local copies, waits for them, and re-layouts: 16.2 us -> none  [the longest x2 5.79 us: local(): tokens[source_row] * filled.astype(jnp.bfloat16)[:, None]]
    scatter x2 -> x0, local copies, waits for them, and re-layouts: 6.76 us -> none  [the longest x1 3.38 us: local(): owner_pair = jnp.zeros((ep_count * slot_count,), jnp.int32).at[target].se...]
    reshape x5 -> x0, local copies, waits for them, and re-layouts: 6.63 us -> none  [the longest x1 1.73 us: local(): arrived_grad = arrived_grad.reshape(-1, feature_width)]
    unnamed x10 -> x11, local copies, waits for them, and re-layouts: 2.66 us -> 8.32 us
  transfers between devices with their start and end apart: 8 -> 0, of which waited for: 4 -> 0; matrix products, arithmetic and copies ran while one was open for 20% -> 0% of each run, Pallas kernels for 0% -> 0%
where the time goes in v1:
time: 110 us; the launch traced here: 109 us
  Pallas kernels  98.4 us (89%)
  local copies, waits for them, and re-layouts  8.32 us (8%)
  other arithmetic  2.05 us (2%)
    pallas_call x1, Pallas kernels, local(): pl.pallas_call(functools.partial(kernel, dims), out_shape=(jax.ShapeDtype...  98.4 us
    unnamed x11, local copies, waits for them, and re-layouts  8.32 us

profile of v1, /device:TPU:0, one launch (start us, length us, event | category | flops | bytes accessed | tf_op | source)
XLA Modules:
  0.0 109.5 jit_solution(3711332910396163788)
XLA Ops:
  0.6 0.0 copy-start.1
  0.6 0.8 convert_bitcast_fusion
  1.4 1.3 %select_maximum_fusion.meta_ref = f32[16,128]{1,0:T(8,128)} fusion(f32[6,128]{1,0:T(8,128)} %bitcast.13, f32[6,128]{1,0:T(8,128)S(1)} %convert_bitcast_fusion), kind=kLoop, calls=%fused_computation | loop fusion | flops 10240 | bytes 14336 | tf_op jit(solution)/shard_map/concatenate | solution.py:316
  2.7 2.3 %copy.10 = bf16[1,512,704]{2,1,0:T(8,128)(2,1)} copy(bf16[1,512,704]{1,2,0:T(8,128)(2,1)} %param.11) | data formatting | bytes 1441792 | tf_op args[4]
  5.0 0.0 copy-done.1
  5.0 1.2 %copy.11 = bf16[1,512,704]{2,1,0:T(8,128)(2,1)} copy(bf16[1,512,704]{1,2,0:T(8,128)(2,1)S(1)} %copy-done.1) | data formatting | bytes 1441792 | tf_op args[5]
  6.1 98.4 %shard_map.94 = (bf16[128,1024]{1,0:T(8,128)(2,1)}, f32[512,704]{1,0:T(8,128)}, f32[704,512]{1,0:T(8,128)}) custom-call(f32[16,128]{1,0:T(8,128)} %select_maximum_fusion.meta_ref, bf16[128,1024]{1,0:T(8,128)(2,1)} %tok_ref.1, bf16[128,1024]{1,0:T(8,128)(2,1)} %cot_ref.1, bf16[512,704]{1,0:T(8,128)(2,1)} %bitcast.8, bf16[512,704]{1,0:T(8,128)(2,1)} %bitcast.9, ...), custom_call_target="tpu_custom_call" | custom-call | tf_op jit(solution)/shard_map/pallas_call | solution.py:327
  104.6 0.0 copy-start.2
  104.6 0.0 copy-start
  104.6 3.1 %copy.12 = f32[1,512,704]{1,2,0:T(8,128)} copy(f32[1,512,704]{2,1,0:T(8,128)} %bitcast.10) | data formatting | bytes 2883584
  107.7 0.0 copy-done.2
  107.7 0.7 copy.15
  108.4 0.0 copy-done
  108.4 1.1 %copy.16 = f32[1,704,512]{2,1,0:T(8,128)} copy(f32[1,704,512]{2,1,0:T(8,128)S(1)} %bitcast.11) | data formatting | bytes 2883584
Async XLA Ops:
  0.6 4.3 %copy-start.1 = (bf16[1,512,704]{1,2,0:T(8,128)(2,1)S(1)}, bf16[1,512,704]{1,2,0:T(8,128)(2,1)}, u32[]{:S(2)}) copy-start(bf16[1,512,704]{1,2,0:T(8,128)(2,1)} %param.12) | copy-start | bytes 2162692
  104.6 3.1 %copy-start.2 = (bf16[128,1024]{1,0:T(8,128)(2,1)S(1)}, bf16[128,1024]{1,0:T(8,128)(2,1)}, u32[]{:S(2)}) copy-start(bf16[128,1024]{1,0:T(8,128)(2,1)} %get-tuple-element.15) | copy-start | bytes 786436
  104.6 3.8 %copy-start = (f32[704,512]{1,0:T(8,128)S(1)}, f32[704,512]{1,0:T(8,128)}, u32[]{:S(2)}) copy-start(f32[704,512]{1,0:T(8,128)} %get-tuple-element.8) | copy-start | bytes 4325380

commit v2 on v1

v2 whole, which is shorter than its diff:
```python
import functools

import jax
import jax.numpy as jnp
from jax import lax
from jax.experimental import pallas as pl
from jax.experimental.pallas import tpu as pltpu
from jax.sharding import PartitionSpec as P

MESH = pl.DeviceIdType.MESH
F32 = jnp.float32
BF16 = jnp.bfloat16


def rows_of(count, unit):
    return -(-count // unit) * unit


def outer_of(ep_count):
    outer = 1
    while outer * outer < ep_count and ep_count % (outer * 2) == 0:
        outer *= 2
    return outer


def contract_columns(lhs, rhs):
    return lax.dot_general(lhs, rhs, (((1,), (1,)), ((), ())), preferred_element_type=F32)


def contract_rows(lhs, rhs):
    return lax.dot_general(lhs, rhs, (((0,), (0,)), ((), ())), preferred_element_type=F32)


def kernel(
    dims,
    meta_ref, tok_ref, cot_ref, wg_ref, wu_ref, wd_ref,
    mixed_ref, gup_ref, gdn_ref,
    metab, tokb, cotb, wgb, wub, wdb,
    slotb, gateb, pick, scale, mixhi, mixlo,
    sendx, recvx, sendg, recvg, sendo, recvo,
    gacc, uacc, hid, upg,
    comb, macc, sendz, recvz, supb, rupb, sdnb, rdnb,
    lsem, zs, zr, fs, ps, pr, ys, yr, ws, wr, gs, gr,
):
    A, B, R, C, T, K, KP, cap, S, D, DC, H, W = dims
    CR = C // R
    ep = lax.axis_index("ep")
    rep = lax.axis_index("rep")
    oa, ob = ep // B, ep % B

    def out_peer(j):
        return {"ep": lax.rem(oa + j, A) * B + ob}

    def in_peer(j):
        return {"ep": oa * B + lax.rem(ob + j + B, B)}

    def rep_peer(j):
        return {"rep": lax.rem(rep + j, R)}

    peers = (
        [out_peer(j) for j in range(1, A)]
        + [in_peer(j) for j in range(1, B)]
        + [rep_peer(j) for j in range(1, R)]
    )

    def build(src, dst, ssem, rsem, peer):
        return pltpu.make_async_remote_copy(
            src_ref=src, dst_ref=dst, send_sem=ssem, recv_sem=rsem,
            device_id=peer, device_id_type=MESH,
        )

    def remote(src, dst, ssem, rsem, peer):
        copy = build(src, dst, ssem, rsem, peer)
        copy.start()
        return copy

    started = []
    local = {}

    def keep(src, dst, index):
        copy = pltpu.make_async_copy(src, dst, lsem.at[index])
        copy.start()
        return copy

    def cols(c):
        return pl.ds(pl.multiple_of(c * DC, 128), DC)

    first = lax.rem(rep + 1, R) * CR
    turn = [lax.rem(first + i, C) for i in range(C)]

    for c in range(C):
        local["t", c] = keep(tok_ref.at[:, cols(c)], tokb.at[c, oa], c)
    local["g"] = keep(wg_ref, wgb.at[rep], 2 * C)
    local["u"] = keep(wu_ref, wub.at[rep], 2 * C + 1)
    local["d"] = keep(wd_ref, wdb.at[rep], 2 * C + 2)
    for i in range(C):
        local["c", i] = keep(cot_ref.at[:, cols(turn[i])], cotb.at[turn[i], oa], C + i)

    barrier = pltpu.get_barrier_semaphore()
    for peer in peers:
        pl.semaphore_signal(barrier, inc=1, device_id=peer, device_id_type=MESH)
    pl.semaphore_wait(barrier, len(peers))

    relay = A > 2
    zc = {}
    fc = {}
    later = []

    def sends_itself(j):
        if relay and j == A - 1:
            return oa != 0
        if relay and j == 1:
            return oa != A - 1
        return None

    def guarded(condition, action):
        if condition is None:
            action()
        else:
            pl.when(condition)(action)

    def spread(k, c, src, buf):
        for j in range(1, A):
            copy = build(src.at[:, cols(c)], buf.at[c, oa], zs.at[k, j], zr.at[k, j], out_peer(j))
            zc[k, j] = copy
            guarded(sends_itself(j), copy.start)
            later.append((sends_itself(j), copy))

    def pass_on(k, c, buf):
        if not relay:
            return
        for n, (at, source, j, last, slot) in enumerate(
            ((A - 2, 0, A - 2, A - 1, A - 1), (1, A - 1, 2, 0, 1))
        ):
            copy = build(
                buf.at[c, source], buf.at[c, source], fs.at[k, n], zr.at[k, slot],
                {"ep": last * B + ob},
            )

            def act(copy=copy, j=j):
                zc[k, j].wait_recv()
                copy.start()

            pl.when(oa == at)(act)
            later.append((oa == at, copy))

    def arrive(k):
        for j in range(1, A):
            condition = None
            if relay and j == A - 2:
                condition = oa != A - 2
            if relay and j == 2:
                other = oa != 1
                condition = other if condition is None else jnp.logical_and(condition, other)
            guarded(condition, zc[k, j].wait_recv)

    mc = {}
    for j in range(1, A):
        mc[j] = remote(meta_ref, metab.at[oa], zs.at[2 * C, j], zr.at[2 * C, j], out_peer(j))
    for c in range(C):
        spread(c, c, tok_ref, tokb)
    wc = {}
    for n, (src, dst) in enumerate(((wg_ref, wgb), (wu_ref, wub), (wd_ref, wdb))):
        for j in range(1, R):
            wc[n, j] = remote(src, dst.at[rep], ws.at[n, j], wr.at[n, j], rep_peer(j))
    started += list(mc.values()) + list(wc.values())

    metab[oa] = meta_ref[...]
    BP = slotb.shape[0]
    row = lax.broadcasted_iota(jnp.int32, (BP, T), 0)
    named = jnp.where(row < B, oa * B + lax.rem(ob + row, B), -1).astype(F32)
    earlier = (
        lax.broadcasted_iota(jnp.int32, (T, T), 0) < lax.broadcasted_iota(jnp.int32, (T, T), 1)
    ).astype(F32).astype(BF16)
    for j in range(1, A):
        mc[j].wait_recv()
    for a in range(A):
        member = jnp.zeros((BP, T), F32)
        weight = jnp.zeros((BP, T), F32)
        for k in range(K):
            same = metab[a, k : k + 1, :] == named
            member = member + jnp.where(same, 1.0, 0.0)
            weight = weight + jnp.where(same, metab[a, KP + k : KP + k + 1, :], 0.0)
        place = jnp.dot(member.astype(BF16), earlier, preferred_element_type=F32)
        slotb[:, a * T : (a + 1) * T] = jnp.where(member > 0.5, place + float(a * cap), -1.0)
        gateb[:, a * T : (a + 1) * T] = weight
    starts = [a * cap // 16 * 16 for a in range(A)]
    slot_id = lax.broadcasted_iota(jnp.int32, (S, A * T), 0).astype(F32)
    for b in range(B):
        hit = slotb[b : b + 1, :] == slot_id
        pick[b] = jnp.where(hit, 1.0, 0.0).astype(BF16)
        mix = jnp.where(hit, gateb[b : b + 1, :], 0.0)
        scale[b] = jnp.sum(mix, axis=1, keepdims=True)
        for a in range(A):
            part = mix[starts[a] : starts[a] + W, a * T : (a + 1) * T]
            high = part.astype(BF16)
            mixhi[a, b] = high
            mixlo[a, b] = (part - high.astype(F32)).astype(BF16)

    pc = {}

    def pack_rows(c):
        local["t", c].wait()
        pass_on(c, c, tokb)
        arrive(c)
        source = tokb[c].reshape(A * T, DC)
        packed = jnp.dot(pick[...].reshape(B * S, A * T), source, preferred_element_type=F32)
        for j in list(range(1, B)) + [0]:
            block = packed[j * S : (j + 1) * S].astype(BF16)
            if j == 0:
                recvx[c, 0] = block
            else:
                sendx[c, j] = block
                pc["x", c, j] = remote(
                    sendx.at[c, j], recvx.at[c, j], ps.at[c, j], pr.at[c, j], in_peer(j)
                )

    def pack_grads(i):
        c = turn[i]
        local["c", i].wait()
        arrive(C + i)
        source = cotb[c].reshape(A * T, DC)
        packed = jnp.dot(pick[...].reshape(B * S, A * T), source, preferred_element_type=F32)
        for j in list(range(1, B)) + [0]:
            block = (packed[j * S : (j + 1) * S] * scale[j]).astype(BF16)
            if j == 0:
                recvg[c, 0] = block
            else:
                sendg[c, j] = block
                pc["g", i, j] = remote(
                    sendg.at[c, j], recvg.at[c, j], ps.at[C + i, j], pr.at[C + i, j], in_peer(j)
                )

    for c in range(C):
        pack_rows(c)
        spread(C + c, turn[c], cot_ref, cotb)

    local["g"].wait()
    local["u"].wait()
    for j in range(1, R):
        wc[0, j].wait_recv()
        wc[1, j].wait_recv()
    for c in range(C):
        part = pl.ds((c % CR) * DC, DC)
        for j in range(1, B):
            pc["x", c, j].wait_recv()

        rows = recvx[c].reshape(B * S, DC)
        gate = contract_columns(rows, wgb[c // CR, :, part])
        up = contract_columns(rows, wub[c // CR, :, part])
        if c > 0:
            gate = gate + gacc[...]
            up = up + uacc[...]
        if c < C - 1:
            gacc[...] = gate
            uacc[...] = up
        else:
            silu = gate / (1.0 + jnp.exp(-gate))
            gacc[...] = silu
            hid[...] = (silu * up).astype(BF16)

    local["d"].wait()
    for j in range(1, R):
        wc[2, j].wait_recv()
    for c in range(C):
        part = pl.ds((c % CR) * DC, DC)
        result = jnp.dot(hid[...], wdb[c // CR, :, part], preferred_element_type=F32)
        for j in list(range(1, B)) + [0]:
            block = result[j * S : (j + 1) * S].astype(BF16)
            if j == 0:
                recvo[c, 0] = block
            else:
                sendo[c, j] = block
                pc["o", c, j] = remote(
                    sendo.at[c, j], recvo.at[c, j],
                    ps.at[2 * C + c, j], pr.at[2 * C + c, j], in_peer(-j),
                )
        pass_on(C + c, turn[c], cotb)

    for i in range(C):
        pack_grads(i)

    yc = {}

    def combine(c):
        for j in range(1, B):
            pc["o", c, j].wait_recv()
        for a in range(A):
            rows = recvo[c, :, pl.ds(starts[a], W), :].reshape(B * W, DC)
            total = contract_rows(mixhi[a].reshape(B * W, T), rows)
            total = total + contract_rows(mixlo[a].reshape(B * W, T), rows)
            comb[a] = total
            sendz[c, a] = total.astype(BF16)
        macc[c] = comb[oa]
        for j in range(1, A):
            yc[c, j] = remote(
                sendz.at[c, lax.rem(oa + j, A)], recvz.at[c, j],
                ys.at[c, j], yr.at[c, j], out_peer(j),
            )

    for c in range(C):
        combine(c)

    def shard(ref, index):
        return jnp.concatenate(
            [ref[index * CR + i].reshape(B * S, DC) for i in range(CR)], axis=1
        )

    gc = {}
    for i in range(C):
        part = pl.ds((i % CR) * DC, DC)
        group = i // CR
        for j in range(1, B):
            pc["g", i, j].wait_recv()
        rows = recvg[turn[i]].reshape(B * S, DC)
        value = contract_columns(rows, wdb[lax.rem(rep + 1 + group, R), :, part])
        if i > 0:
            value = value + uacc[...]
        if i < C - 1:
            uacc[...] = value
        else:
            upg[...] = (value * gacc[...]).astype(BF16)
        if i == C - 1:
            for j in range(1, R):
                peer = lax.rem(rep + j, R)
                supb[j] = contract_rows(upg[...], shard(recvx, peer)).astype(BF16)
                gc[0, j] = remote(supb.at[j], rupb.at[j], gs.at[0, j], gr.at[0, j], rep_peer(j))
        block = contract_rows(hid[...], rows).astype(BF16)
        if group < R - 1:
            j = group + 1
            sdnb[j, :, part] = block
            if i % CR == CR - 1:
                gc[1, j] = remote(sdnb.at[j], rdnb.at[j], gs.at[1, j], gr.at[1, j], rep_peer(j))
        else:
            gdn_ref[:, part] = block.astype(F32)

    gup_ref[...] = contract_rows(upg[...], shard(recvx, rep)).astype(BF16).astype(F32)
    for j in range(1, R):
        gc[0, j].wait_recv()
        gup_ref[...] += rupb[j].astype(F32)
        gc[1, j].wait_recv()
        gdn_ref[...] += rdnb[j].astype(F32)

    for c in range(C):
        total = macc[c]
        for j in range(1, A):
            yc[c, j].wait_recv()
            total = total + recvz[c, j].astype(F32)
        mixed_ref[:, c * DC : (c + 1) * DC] = total.astype(BF16)

    started += list(pc.values()) + list(gc.values()) + list(yc.values())
    for copy in started:
        copy.wait_send()
    for condition, copy in later:
        guarded(condition, copy.wait_send)


def local(tokens, expert_ids, gate_weights, cotangent, w_gate, w_up, w_down):
    ep_count, R = lax.axis_size("ep"), lax.axis_size("rep")
    T, D = tokens.shape
    K = expert_ids.shape[1]
    H = w_gate.shape[2]
    cap = T * K // ep_count + 1
    A = outer_of(ep_count)
    B = ep_count // A
    W = max(rows_of((a + 1) * cap, 16) - a * cap // 16 * 16 for a in range(A))
    S = max(a * cap // 16 * 16 for a in range(A)) + W
    DR = D // R
    DC = DR // 2 if DR % 256 == 0 else DR
    C = D // DC
    KP = rows_of(K, 8)
    BP = rows_of(B, 16)
    meta = jnp.concatenate(
        [
            jnp.pad(expert_ids.T.astype(F32), ((0, KP - K), (0, 0)), constant_values=-2.0),
            jnp.pad(gate_weights.T, ((0, KP - K), (0, 0))),
        ]
    )
    dims = (A, B, R, C, T, K, KP, cap, S, D, DC, H, W)
    vmem, dma = pltpu.VMEM, pltpu.SemaphoreType.DMA
    anywhere = pl.BlockSpec(memory_space=pl.ANY)
    inside = pl.BlockSpec(memory_space=pltpu.VMEM)
    blocks = vmem((C, B, S, DC), BF16)
    mixed, gup, gdn = pl.pallas_call(
        functools.partial(kernel, dims),
        out_shape=(
            jax.ShapeDtypeStruct((T, D), BF16),
            jax.ShapeDtypeStruct((H, DR), F32),
            jax.ShapeDtypeStruct((H, DR), F32),
        ),
        in_specs=[inside] + [anywhere] * 5,
        out_specs=[inside] * 3,
        scratch_shapes=[
            vmem((A, 2 * KP, T), F32),
            vmem((C, A, T, DC), BF16),
            vmem((C, A, T, DC), BF16),
            vmem((R, H, DR), BF16),
            vmem((R, H, DR), BF16),
            vmem((R, H, DR), BF16),
            vmem((BP, A * T), F32),
            vmem((BP, A * T), F32),
            vmem((B, S, A * T), BF16),
            vmem((B, S, 1), F32),
            vmem((A, B, W, T), BF16),
            vmem((A, B, W, T), BF16),
            blocks, blocks, blocks, blocks, blocks, blocks,
            vmem((B * S, H), F32),
            vmem((B * S, H), F32),
            vmem((B * S, H), BF16),
            vmem((B * S, H), BF16),
            vmem((A, T, DC), F32),
            vmem((C, T, DC), F32),
            vmem((C, A, T, DC), BF16),
            vmem((C, A, T, DC), BF16),
            vmem((R, H, DR), BF16),
            vmem((R, H, DR), BF16),
            vmem((R, H, DR), BF16),
            vmem((R, H, DR), BF16),
            dma((2 * C + 3,)),
            dma((2 * C + 1, A)), dma((2 * C + 1, A)),
            dma((2 * C, 2)),
            dma((3 * C, B)), dma((3 * C, B)),
            dma((C, A)), dma((C, A)),
            dma((3, R)), dma((3, R)),
            dma((2, R)), dma((2, R)),
        ],
        compiler_params=pltpu.CompilerParams(
            collective_id=0, has_side_effects=True, vmem_limit_bytes=62 * 1024 * 1024
        ),
    )(meta, tokens, cotangent, w_gate[0].T, w_up[0].T, w_down[0])
    return mixed, gup.T[None], gdn[None]


def solution(mesh):
    in_specs = (
        P(("ep", "rep"), None),
        P(("ep", "rep"), None),
        P(("ep", "rep"), None),
        P(("ep", "rep"), None),
        P("ep", "rep", None),
        P("ep", "rep", None),
        P("ep", None, "rep"),
    )
    out_specs = (P(("ep", "rep"), None), P("ep", "rep", None), P("ep", None, "rep"))
    return jax.shard_map(local, mesh=mesh, in_specs=in_specs, out_specs=out_specs, check_vma=False)
```

time: 110 us -> 92.9 us (0.84)
  Pallas kernels: 98.4 us -> 84.5 us
  local copies, waits for them, and re-layouts: 8.32 us -> 5.45 us
    pallas_call x1, Pallas kernels: 98.4 us -> 84.5 us  [local(): pl.pallas_call(functools.partial(kernel, dims), out_shape=(jax.ShapeDtype...]
    unnamed x11 -> x5, local copies, waits for them, and re-layouts: 8.32 us -> 5.45 us
where the time goes in v2:
time: 92.9 us; the launch traced here: 92.5 us
  Pallas kernels  84.5 us (91%)
  local copies, waits for them, and re-layouts  5.45 us (6%)
  other arithmetic  1.98 us (2%)
    pallas_call x1, Pallas kernels, local(): pl.pallas_call(functools.partial(kernel, dims), out_shape=(jax.ShapeDtype...  84.5 us
    unnamed x5, local copies, waits for them, and re-layouts  5.45 us

profile of v2, /device:TPU:0, one launch (start us, length us, event | category | flops | bytes accessed | tf_op | source)
XLA Modules:
  0.0 92.5 jit_solution(18167360981656743265)
XLA Ops:
  0.6 0.7 convert_bitcast_fusion
  1.3 1.3 %select_maximum_fusion.meta_ref = f32[16,128]{1,0:T(8,128)} fusion(f32[6,128]{1,0:T(8,128)} %bitcast.19, f32[6,128]{1,0:T(8,128)S(1)} %convert_bitcast_fusion), kind=kLoop, calls=%fused_computation | loop fusion | flops 10240 | bytes 14336 | tf_op jit(solution)/shard_map/concatenate | solution.py:373
  2.6 84.5 %shard_map.94 = (bf16[128,1024]{1,0:T(8,128)(2,1)}, f32[704,512]{1,0:T(8,128)}, f32[704,512]{1,0:T(8,128)}) custom-call(f32[16,128]{1,0:T(8,128)} %select_maximum_fusion.meta_ref, bf16[128,1024]{1,0:T(8,128)(2,1)} %tok_ref.1, bf16[128,1024]{1,0:T(8,128)(2,1)} %cot_ref.1, bf16[704,512]{1,0:T(8,128)(2,1)} %bitcast.16, bf16[704,512]{1,0:T(8,128)(2,1)} %bitcast.17, ...), custom_call_target="tpu_custom_call" | custom-call | tf_op jit(solution)/shard_map/pallas_call | solution.py:384
  87.1 1.7 %copy.13 = bf16[128,1024]{1,0:T(8,128)(2,1)} copy(bf16[128,1024]{1,0:T(8,128)(2,1)} %get-tuple-element.12) | data formatting | bytes 524288
  88.8 0.0 copy-start
  88.8 2.7 %copy.14 = f32[1,512,704]{1,2,0:T(8,128)} copy(f32[1,512,704]{1,2,0:T(8,128)} %bitcast.15) | data formatting | bytes 2883584
  91.4 0.0 copy-done
  91.4 1.1 %copy.15 = f32[1,704,512]{2,1,0:T(8,128)} copy(f32[1,704,512]{2,1,0:T(8,128)S(1)} %bitcast.14) | data formatting | bytes 2883584
Async XLA Ops:
  88.8 2.7 %copy-start = (f32[704,512]{1,0:T(8,128)S(1)}, f32[704,512]{1,0:T(8,128)}, u32[]{:S(2)}) copy-start(f32[704,512]{1,0:T(8,128)} %get-tuple-element.8) | copy-start | bytes 4325380

commit v3 on v2

--- a/solution.py
+++ b/solution.py
@@ -10,6 +10,7 @@
 MESH = pl.DeviceIdType.MESH
 F32 = jnp.float32
 BF16 = jnp.bfloat16
+VMEM_MIB = 60
 
 
 def rows_of(count, unit):
@@ -33,16 +34,16 @@
 
 def kernel(
     dims,
-    meta_ref, tok_ref, cot_ref, wg_ref, wu_ref, wd_ref,
+    ids_ref, weight_ref, tok_ref, cot_ref, wg_ref, wu_ref, wd_ref,
     mixed_ref, gup_ref, gdn_ref,
-    metab, tokb, cotb, wgb, wub, wdb,
+    idb, weightb, tokb, cotb, wgb, wub, wdb,
     slotb, gateb, pick, scale, mixhi, mixlo,
     sendx, recvx, sendg, recvg, sendo, recvo,
     gacc, uacc, hid, upg,
     comb, macc, sendz, recvz, supb, rupb, sdnb, rdnb,
     lsem, zs, zr, fs, ps, pr, ys, yr, ws, wr, gs, gr,
 ):
-    A, B, R, C, T, K, KP, cap, S, D, DC, H, W = dims
+    A, B, R, C, T, K, cap, S, D, DC, H, W = dims
     CR = C // R
     ep = lax.axis_index("ep")
     rep = lax.axis_index("rep")
@@ -156,7 +157,10 @@
 
     mc = {}
     for j in range(1, A):
-        mc[j] = remote(meta_ref, metab.at[oa], zs.at[2 * C, j], zr.at[2 * C, j], out_peer(j))
+        for n, (src, dst) in enumerate(((ids_ref, idb), (weight_ref, weightb))):
+            mc[n, j] = remote(
+                src, dst.at[oa], zs.at[2 * C + n, j], zr.at[2 * C + n, j], out_peer(j)
+            )
     for c in range(C):
         spread(c, c, tok_ref, tokb)
     wc = {}
@@ -165,22 +169,24 @@
             wc[n, j] = remote(src, dst.at[rep], ws.at[n, j], wr.at[n, j], rep_peer(j))
     started += list(mc.values()) + list(wc.values())
 
-    metab[oa] = meta_ref[...]
+    idb[oa] = ids_ref[...]
+    weightb[oa] = weight_ref[...]
     BP = slotb.shape[0]
     row = lax.broadcasted_iota(jnp.int32, (BP, T), 0)
-    named = jnp.where(row < B, oa * B + lax.rem(ob + row, B), -1).astype(F32)
+    named = jnp.where(row < B, oa * B + lax.rem(ob + row, B), -1)
     earlier = (
         lax.broadcasted_iota(jnp.int32, (T, T), 0) < lax.broadcasted_iota(jnp.int32, (T, T), 1)
     ).astype(F32).astype(BF16)
     for j in range(1, A):
-        mc[j].wait_recv()
+        mc[0, j].wait_recv()
+        mc[1, j].wait_recv()
     for a in range(A):
         member = jnp.zeros((BP, T), F32)
         weight = jnp.zeros((BP, T), F32)
         for k in range(K):
-            same = metab[a, k : k + 1, :] == named
+            same = idb[a, k : k + 1, :] == named
             member = member + jnp.where(same, 1.0, 0.0)
-            weight = weight + jnp.where(same, metab[a, KP + k : KP + k + 1, :], 0.0)
+            weight = weight + jnp.where(same, weightb[a, k : k + 1, :], 0.0)
         place = jnp.dot(member.astype(BF16), earlier, preferred_element_type=F32)
         slotb[:, a * T : (a + 1) * T] = jnp.where(member > 0.5, place + float(a * cap), -1.0)
         gateb[:, a * T : (a + 1) * T] = weight
@@ -242,6 +248,9 @@
         wc[1, j].wait_recv()
     for c in range(C):
         part = pl.ds((c % CR) * DC, DC)
+        if c == C - 1:
+            pass_on(C, turn[0], cotb)
+            pack_grads(0)
         for j in range(1, B):
             pc["x", c, j].wait_recv()
 
@@ -275,9 +284,10 @@
                     sendo.at[c, j], recvo.at[c, j],
                     ps.at[2 * C + c, j], pr.at[2 * C + c, j], in_peer(-j),
                 )
-        pass_on(C + c, turn[c], cotb)
-
-    for i in range(C):
+        if c > 0:
+            pass_on(C + c, turn[c], cotb)
+
+    for i in range(1, C):
         pack_grads(i)
 
     yc = {}
@@ -298,16 +308,14 @@
                 ys.at[c, j], yr.at[c, j], out_peer(j),
             )
 
-    for c in range(C):
-        combine(c)
-
     def shard(ref, index):
         return jnp.concatenate(
             [ref[index * CR + i].reshape(B * S, DC) for i in range(CR)], axis=1
         )
 
     gc = {}
-    for i in range(C):
+
+    def back(i):
         part = pl.ds((i % CR) * DC, DC)
         group = i // CR
         for j in range(1, B):
@@ -334,6 +342,12 @@
         else:
             gdn_ref[:, part] = block.astype(F32)
 
+    back(0)
+    for c in range(C):
+        combine(c)
+        if c > 0:
+            back(c)
+
     gup_ref[...] = contract_rows(upg[...], shard(recvx, rep)).astype(BF16).astype(F32)
     for j in range(1, R):
         gc[0, j].wait_recv()
@@ -368,15 +382,8 @@
     DR = D // R
     DC = DR // 2 if DR % 256 == 0 else DR
     C = D // DC
-    KP = rows_of(K, 8)
     BP = rows_of(B, 16)
-    meta = jnp.concatenate(
-        [
-            jnp.pad(expert_ids.T.astype(F32), ((0, KP - K), (0, 0)), constant_values=-2.0),
-            jnp.pad(gate_weights.T, ((0, KP - K), (0, 0))),
-        ]
-    )
-    dims = (A, B, R, C, T, K, KP, cap, S, D, DC, H, W)
+    dims = (A, B, R, C, T, K, cap, S, D, DC, H, W)
     vmem, dma = pltpu.VMEM, pltpu.SemaphoreType.DMA
     anywhere = pl.BlockSpec(memory_space=pl.ANY)
     inside = pl.BlockSpec(memory_space=pltpu.VMEM)
@@ -388,10 +395,11 @@
             jax.ShapeDtypeStruct((H, DR), F32),
             jax.ShapeDtypeStruct((H, DR), F32),
         ),
-        in_specs=[inside] + [anywhere] * 5,
+        in_specs=[inside] * 2 + [anywhere] * 5,
         out_specs=[inside] * 3,
         scratch_shapes=[
-            vmem((A, 2 * KP, T), F32),
+            vmem((A, K, T), jnp.int32),
+            vmem((A, K, T), F32),
             vmem((C, A, T, DC), BF16),
             vmem((C, A, T, DC), BF16),
             vmem((R, H, DR), BF16),
@@ -417,7 +425,7 @@
             vmem((R, H, DR), BF16),
             vmem((R, H, DR), BF16),
             dma((2 * C + 3,)),
-            dma((2 * C + 1, A)), dma((2 * C + 1, A)),
+            dma((2 * C + 2, A)), dma((2 * C + 2, A)),
             dma((2 * C, 2)),
             dma((3 * C, B)), dma((3 * C, B)),
             dma((C, A)), dma((C, A)),
@@ -425,9 +433,9 @@
             dma((2, R)), dma((2, R)),
         ],
         compiler_params=pltpu.CompilerParams(
-            collective_id=0, has_side_effects=True, vmem_limit_bytes=62 * 1024 * 1024
+            collective_id=0, has_side_effects=True, vmem_limit_bytes=VMEM_MIB * 1024 * 1024
         ),
-    )(meta, tokens, cotangent, w_gate[0].T, w_up[0].T, w_down[0])
+    )(expert_ids.T, gate_weights.T, tokens, cotangent, w_gate[0].T, w_up[0].T, w_down[0])
     return mixed, gup.T[None], gdn[None]
 
 

time: 92.9 us -> 88.4 us (0.952)
  Pallas kernels: 84.5 us -> 82.1 us
  other arithmetic: 1.98 us -> 0 us
    pallas_call x1, Pallas kernels: 84.5 us -> 82.1 us  [local(): pl.pallas_call(functools.partial(kernel, dims), out_shape=(jax.ShapeDtype...]
    concatenate x1 -> x0, other arithmetic: 1.29 us -> none  [local(): jnp.concatenate([jnp.pad(expert_ids.T.astype(F32), ((0, KP - K), (0, 0)),...]
where the time goes in v3:
time: 88.4 us; the launch traced here: 88.2 us
  Pallas kernels  82.1 us (93%)
  local copies, waits for them, and re-layouts  5.45 us (6%)
    pallas_call x1, Pallas kernels, local(): pl.pallas_call(functools.partial(kernel, dims), out_shape=(jax.ShapeDtype...  82.1 us
    unnamed x5, local copies, waits for them, and re-layouts  5.45 us

profile of v3, /device:TPU:0, one launch (start us, length us, event | category | flops | bytes accessed | tf_op | source)
XLA Modules:
  0.0 88.2 jit_solution(15848004515871249450)
XLA Ops:
  0.6 82.1 %shard_map.94 = (bf16[128,1024]{1,0:T(8,128)(2,1)}, f32[704,512]{1,0:T(8,128)}, f32[704,512]{1,0:T(8,128)}) custom-call(s32[6,128]{1,0:T(8,128)} %bitcast.18, f32[6,128]{1,0:T(8,128)} %bitcast.19, bf16[128,1024]{1,0:T(8,128)(2,1)} %tok_ref.1, bf16[128,1024]{1,0:T(8,128)(2,1)} %cot_ref.1, bf16[704,512]{1,0:T(8,128)(2,1)} %bitcast.15, ...), custom_call_target="tpu_custom_call" | custom-call | tf_op jit(solution)/shard_map/pallas_call | solution.py:391
  82.7 1.7 %copy.13 = bf16[128,1024]{1,0:T(8,128)(2,1)} copy(bf16[128,1024]{1,0:T(8,128)(2,1)} %get-tuple-element.12) | data formatting | bytes 524288
  84.4 0.0 copy-start
  84.4 2.7 %copy.14 = f32[1,512,704]{1,2,0:T(8,128)} copy(f32[1,512,704]{1,2,0:T(8,128)} %bitcast.14) | data formatting | bytes 2883584
  87.1 0.0 copy-done
  87.1 1.1 %copy.15 = f32[1,704,512]{2,1,0:T(8,128)} copy(f32[1,704,512]{2,1,0:T(8,128)S(1)} %bitcast.13) | data formatting | bytes 2883584
Async XLA Ops:
  84.4 2.7 %copy-start = (f32[704,512]{1,0:T(8,128)S(1)}, f32[704,512]{1,0:T(8,128)}, u32[]{:S(2)}) copy-start(f32[704,512]{1,0:T(8,128)} %get-tuple-element.8) | copy-start | bytes 4325380
